TPU v7x, 32 devices: a whole 2x2x4 slice. The times are simulated.
32 devices in a mesh: wide: 16 (over z, y, core), narrow: 2 (over x).
Axes of the slice: x: 2, y: 2, z: 4, core: 2. Of those that a mesh axis runs over, the one named last changes fastest.
Arguments:
- block_input: float32 [32, 2, 256, 1152], P(('wide', 'narrow')), may hold values from -6 to 6
- text: float32 [32, 120, 1152], P(('wide', 'narrow')), may hold values from -6 to 6
- modulation: float32 [32, 6, 1152], P(('wide', 'narrow')), may hold values from -2 to 2
- text_lengths: int32 [32], P(('wide', 'narrow')), may hold values from 1 to 120, as said below
- bucket: int32 [32], P(('wide', 'narrow')), may hold values from 0 to 1
- frames: int32 [32], P(('wide', 'narrow')), may hold values from 1 to 2
- cotangent: float32 [32, 2, 256, 1152], P(('wide', 'narrow')), may hold values from -6 to 6
- spatialqkv: float32 [1152, 3456], P('narrow', 'wide'), may hold values from -0.1875 to 0.1875
- spatialout: float32 [1152, 1152], P('narrow', 'wide'), may hold values from -0.75 to 0.75
- temporalqkv: float32 [1152, 3456], P('narrow', 'wide'), may hold values from -0.1875 to 0.1875
- temporalout: float32 [1152, 1152], P('narrow', 'wide'), may hold values from -0.1875 to 0.1875
- crossquery: float32 [1152, 1152], P('narrow', 'wide'), may hold values from -0.1875 to 0.1875
- crosskeyval: float32 [1152, 2304], P('narrow', 'wide'), may hold values from -0.1875 to 0.1875
- crossout: float32 [1152, 1152], P('narrow', 'wide'), may hold values from -0.375 to 0.375
- feedup: float32 [1152, 4608], P('narrow', 'wide'), may hold values from -0.1875 to 0.1875
- feeddown: float32 [4608, 1152], P('narrow', 'wide'), may hold values from -0.125 to 0.125
- vectors: float32 [16, 1152], P('narrow', 'wide'), may hold values from -2 to 2
- feedbias: float32 [4608], P(('wide', 'narrow')), may hold values from -2 to 2
Outputs:
- block_output: float32 [32, 2, 256, 1152], P(('wide', 'narrow'))
- input_grad: float32 [32, 2, 256, 1152], P(('wide', 'narrow'))
- text_grad: float32 [32, 120, 1152], P(('wide', 'narrow'))
- spatialqkv_grad: float32 [1152, 3456], P('narrow', 'wide')
- spatialout_grad: float32 [1152, 1152], P('narrow', 'wide')
- temporalqkv_grad: float32 [1152, 3456], P('narrow', 'wide')
- temporalout_grad: float32 [1152, 1152], P('narrow', 'wide')
- crossquery_grad: float32 [1152, 1152], P('narrow', 'wide')
- crosskeyval_grad: float32 [1152, 2304], P('narrow', 'wide')
- crossout_grad: float32 [1152, 1152], P('narrow', 'wide')
- feedup_grad: float32 [1152, 4608], P('narrow', 'wide')
- feeddown_grad: float32 [4608, 1152], P('narrow', 'wide')
- vectors_grad: float32 [16, 1152], P('narrow', 'wide')
- feedbias_grad: float32 [4608], P(('wide', 'narrow'))
Inputs may be any that keep to these rules, and one draw needn't show every extreme that they name: `text_lengths`: some sample uses all 120 text tokens. `frames`: read only where bucket is 0.
All inputs are finite; a program needn't handle non-finite values.
Results may differ from a plain program's by a relative error of at most 0.039.
Values may be sent and summed in bfloat16 or wider, within the bound.
A program may use at most 320 MiB of HBM per device.

v0:
```python
from functools import partial

import jax
import jax.numpy as jnp
from jax import lax
from jax.sharding import PartitionSpec as P

HEADS = 16
HEAD = 72
PATCH = 256
FRAMES = 2


def layer_norm(value):
    mean = jnp.mean(value, axis=-1, keepdims=True)
    centered = value - mean
    variance = jnp.mean(centered * centered, axis=-1, keepdims=True)
    return centered * lax.rsqrt(variance + 1e-06)


def modulate(value, shift, scale):
    return layer_norm(value) * (1.0 + scale) + shift


def softmax_rows(scores):
    top = jnp.max(scores, axis=-1, keepdims=True)
    powers = jnp.exp(scores - top)
    return powers / jnp.sum(powers, axis=-1, keepdims=True)


def temporal_mix(projected, pair):
    width = HEADS * HEAD
    split = [
        projected[:, index * width : (index + 1) * width].reshape(FRAMES, -1, HEADS, HEAD)
        for index in range(3)
    ]
    scores = jnp.einsum(
        "rphe,sphe->phrs", split[0], split[1], precision=lax.Precision.HIGHEST
    ) * HEAD ** (-0.5)
    scores = jnp.where(pair, scores, -1000000000.0)
    mixed = jnp.einsum(
        "phrs,sphe->rphe", softmax_rows(scores), split[2], precision=lax.Precision.HIGHEST
    )
    return mixed.reshape(-1, width)


def product(left, right):
    return jnp.dot(left, right, preferred_element_type=jnp.float32)


def transposed(left, right):
    return lax.dot_general(
        left, right, (((0,), (0,)), ((), ())), preferred_element_type=jnp.float32
    )


def against(left, right):
    return lax.dot_general(
        left, right, (((1,), (1,)), ((), ())), preferred_element_type=jnp.float32
    )


def column_sum(value):
    return jnp.sum(value, axis=0, dtype=jnp.float32)


def spatial_mask(kind, tokens):
    segment = jnp.where(kind == 0, jnp.arange(tokens) // PATCH, 0)
    return segment[:, None] == segment[None, :]


def frame_pairs(kind, count):
    return jnp.eye(FRAMES, dtype=bool) | (kind == 0) & (count == 2)


def masked_scores(queries, keys, allowed):
    scores = jnp.einsum(
        "lhe,mhe->hlm", queries, keys, preferred_element_type=jnp.float32
    ) * HEAD ** (-0.5)
    return jnp.where(allowed[None], scores, -1000000000.0)


def attend_forward(queries, keys, values, allowed):
    scores = masked_scores(queries, keys, allowed)
    top = jnp.max(scores, axis=-1, keepdims=True)
    powers = jnp.exp(scores - top)
    total = jnp.sum(powers, axis=-1, keepdims=True)
    probs = (powers / total).astype(jnp.bfloat16)
    mixed = jnp.einsum("hlm,mhe->lhe", probs, values, preferred_element_type=jnp.float32)
    return (mixed, top + jnp.log(total))


def attend_backward(queries, keys, values, allowed, logsum, upstream):
    scale = HEAD ** (-0.5)
    probs = jnp.exp(masked_scores(queries, keys, allowed) - logsum)
    through = jnp.einsum("lhe,mhe->hlm", upstream, values, preferred_element_type=jnp.float32)
    inner = jnp.sum(probs * through, axis=-1, keepdims=True)
    slopes = (probs * (through - inner)).astype(jnp.bfloat16)
    d_queries = (
        jnp.einsum("hlm,mhe->lhe", slopes, keys, preferred_element_type=jnp.float32) * scale
    ).astype(jnp.bfloat16)
    d_keys = (
        jnp.einsum("hlm,lhe->mhe", slopes, queries, preferred_element_type=jnp.float32) * scale
    ).astype(jnp.bfloat16)
    d_values = jnp.einsum(
        "hlm,lhe->mhe", probs.astype(jnp.bfloat16), upstream, preferred_element_type=jnp.float32
    ).astype(jnp.bfloat16)
    return (d_queries, d_keys, d_values)


def collect(pieces):
    part = (
        lax.all_gather(pieces[0], "narrow", axis=0, tiled=True),
        lax.all_gather(pieces[1], "narrow", axis=0, tiled=True),
        lax.all_gather(pieces[2], "narrow", axis=0, tiled=True),
        lax.all_gather(pieces[3], "narrow", axis=0, tiled=True),
        lax.all_gather(pieces[4], "narrow", axis=0, tiled=True),
        lax.all_gather(pieces[5], "narrow", axis=0, tiled=True),
        lax.all_gather(pieces[6], "narrow", axis=0, tiled=True),
        lax.all_gather(pieces[7], "narrow", axis=0, tiled=True),
        lax.all_gather(pieces[8], "narrow", axis=0, tiled=True),
        lax.all_gather(pieces[9], "narrow", axis=0, tiled=True),
        lax.all_gather(pieces[10], "narrow", axis=0, tiled=True),
    )
    return (
        lax.all_gather(part[0], "wide", axis=1, tiled=True),
        lax.all_gather(part[1], "wide", axis=1, tiled=True),
        lax.all_gather(part[2], "wide", axis=1, tiled=True),
        lax.all_gather(part[3], "wide", axis=1, tiled=True),
        lax.all_gather(part[4], "wide", axis=1, tiled=True),
        lax.all_gather(part[5], "wide", axis=1, tiled=True),
        lax.all_gather(part[6], "wide", axis=1, tiled=True),
        lax.all_gather(part[7], "wide", axis=1, tiled=True),
        lax.all_gather(part[8], "wide", axis=1, tiled=True),
        lax.all_gather(part[9], "wide", axis=1, tiled=True),
        lax.all_gather(part[10], "wide", axis=0, tiled=True),
    )


def recollect(pieces):
    part = (
        lax.all_gather(pieces[0], "narrow", axis=0, tiled=True),
        lax.all_gather(pieces[1], "narrow", axis=0, tiled=True),
        lax.all_gather(pieces[2], "narrow", axis=0, tiled=True),
        lax.all_gather(pieces[3], "narrow", axis=0, tiled=True),
        lax.all_gather(pieces[4], "narrow", axis=0, tiled=True),
        lax.all_gather(pieces[5], "narrow", axis=0, tiled=True),
        lax.all_gather(pieces[6], "narrow", axis=0, tiled=True),
        lax.all_gather(pieces[7], "narrow", axis=0, tiled=True),
        lax.all_gather(pieces[8], "narrow", axis=0, tiled=True),
        lax.all_gather(pieces[9], "narrow", axis=0, tiled=True),
        lax.all_gather(pieces[10], "narrow", axis=0, tiled=True),
    )
    return (
        lax.all_gather(part[0], "wide", axis=1, tiled=True),
        lax.all_gather(part[1], "wide", axis=1, tiled=True),
        lax.all_gather(part[2], "wide", axis=1, tiled=True),
        lax.all_gather(part[3], "wide", axis=1, tiled=True),
        lax.all_gather(part[4], "wide", axis=1, tiled=True),
        lax.all_gather(part[5], "wide", axis=1, tiled=True),
        lax.all_gather(part[6], "wide", axis=1, tiled=True),
        lax.all_gather(part[7], "wide", axis=1, tiled=True),
        lax.all_gather(part[8], "wide", axis=1, tiled=True),
        lax.all_gather(part[9], "wide", axis=1, tiled=True),
        lax.all_gather(part[10], "wide", axis=0, tiled=True),
    )


def spread(grads):
    part = (
        lax.psum_scatter(
            grads[0].astype(jnp.bfloat16), "wide", scatter_dimension=1, tiled=True
        ).astype(jnp.float32),
        lax.psum_scatter(
            grads[1].astype(jnp.bfloat16), "wide", scatter_dimension=1, tiled=True
        ).astype(jnp.float32),
        lax.psum_scatter(
            grads[2].astype(jnp.bfloat16), "wide", scatter_dimension=1, tiled=True
        ).astype(jnp.float32),
        lax.psum_scatter(
            grads[3].astype(jnp.bfloat16), "wide", scatter_dimension=1, tiled=True
        ).astype(jnp.float32),
        lax.psum_scatter(
            grads[4].astype(jnp.bfloat16), "wide", scatter_dimension=1, tiled=True
        ).astype(jnp.float32),
        lax.psum_scatter(
            grads[5].astype(jnp.bfloat16), "wide", scatter_dimension=1, tiled=True
        ).astype(jnp.float32),
        lax.psum_scatter(
            grads[6].astype(jnp.bfloat16), "wide", scatter_dimension=1, tiled=True
        ).astype(jnp.float32),
        lax.psum_scatter(
            grads[7].astype(jnp.bfloat16), "wide", scatter_dimension=1, tiled=True
        ).astype(jnp.float32),
        lax.psum_scatter(
            grads[8].astype(jnp.bfloat16), "wide", scatter_dimension=1, tiled=True
        ).astype(jnp.float32),
        lax.psum_scatter(
            grads[9].astype(jnp.bfloat16), "wide", scatter_dimension=1, tiled=True
        ).astype(jnp.float32),
        lax.psum_scatter(
            grads[10].astype(jnp.bfloat16), "wide", scatter_dimension=0, tiled=True
        ).astype(jnp.float32),
    )
    return (
        lax.psum_scatter(
            part[0].astype(jnp.bfloat16), "narrow", scatter_dimension=0, tiled=True
        ).astype(jnp.float32),
        lax.psum_scatter(
            part[1].astype(jnp.bfloat16), "narrow", scatter_dimension=0, tiled=True
        ).astype(jnp.float32),
        lax.psum_scatter(
            part[2].astype(jnp.bfloat16), "narrow", scatter_dimension=0, tiled=True
        ).astype(jnp.float32),
        lax.psum_scatter(
            part[3].astype(jnp.bfloat16), "narrow", scatter_dimension=0, tiled=True
        ).astype(jnp.float32),
        lax.psum_scatter(
            part[4].astype(jnp.bfloat16), "narrow", scatter_dimension=0, tiled=True
        ).astype(jnp.float32),
        lax.psum_scatter(
            part[5].astype(jnp.bfloat16), "narrow", scatter_dimension=0, tiled=True
        ).astype(jnp.float32),
        lax.psum_scatter(
            part[6].astype(jnp.bfloat16), "narrow", scatter_dimension=0, tiled=True
        ).astype(jnp.float32),
        lax.psum_scatter(
            part[7].astype(jnp.bfloat16), "narrow", scatter_dimension=0, tiled=True
        ).astype(jnp.float32),
        lax.psum_scatter(
            part[8].astype(jnp.bfloat16), "narrow", scatter_dimension=0, tiled=True
        ).astype(jnp.float32),
        lax.psum_scatter(
            part[9].astype(jnp.bfloat16), "narrow", scatter_dimension=0, tiled=True
        ).astype(jnp.float32),
        lax.psum_scatter(
            part[10].astype(jnp.bfloat16), "narrow", scatter_dimension=0, tiled=True
        ).astype(jnp.float32),
    )


def clip_forward(weights, block, words, table_in, length, kind, count):
    (
        spatial_in,
        spatial_out,
        temporal_in,
        temporal_out,
        cross_query,
        cross_keyval,
        cross_out,
        feed_up,
        feed_down,
        vectors,
        feed_bias,
    ) = weights
    tokens = FRAMES * PATCH
    width = HEADS * HEAD
    rows = vectors.astype(jnp.float32)
    table = rows[0:6] + table_in
    blank = jnp.zeros((width,), jnp.float32)
    flat = block.reshape(tokens, width)
    entered = modulate(flat, table[0], table[1]).astype(jnp.bfloat16)
    packed = (
        (product(entered, spatial_in) + jnp.concatenate([rows[6], blank, rows[7]]))
        .astype(jnp.bfloat16)
        .reshape(tokens, 3, HEADS, HEAD)
    )
    mixed, spatial_sum = attend_forward(
        packed[:, 0], packed[:, 1], packed[:, 2], spatial_mask(kind, tokens)
    )
    attended = mixed.reshape(tokens, width).astype(jnp.bfloat16)
    spatial = product(attended, spatial_out) + rows[8]
    first = flat + table[2] * spatial
    temporal_proj = product(first.astype(jnp.bfloat16), temporal_in) + jnp.concatenate(
        [rows[9], blank, rows[10]]
    )
    temporal_att = temporal_mix(temporal_proj, frame_pairs(kind, count)).astype(jnp.bfloat16)
    temporal = product(temporal_att, temporal_out) + rows[11]
    second = first + table[2] * temporal
    query_text = (
        (product(second.astype(jnp.bfloat16), cross_query) + rows[12])
        .astype(jnp.bfloat16)
        .reshape(tokens, HEADS, HEAD)
    )
    keyval = (
        (product(words.astype(jnp.bfloat16), cross_keyval) + jnp.concatenate([blank, rows[13]]))
        .astype(jnp.bfloat16)
        .reshape(-1, 2, HEADS, HEAD)
    )
    text_mask = (jnp.arange(words.shape[0]) < length)[None, :]
    mixed, cross_sum = attend_forward(query_text, keyval[:, 0], keyval[:, 1], text_mask)
    cross_att = mixed.reshape(tokens, width).astype(jnp.bfloat16)
    third = second + (product(cross_att, cross_out) + rows[14])
    normed = modulate(third, table[3], table[4]).astype(jnp.bfloat16)
    hidden = product(normed, feed_up) + feed_bias.astype(jnp.float32)
    activated = jax.nn.gelu(hidden, approximate=True).astype(jnp.bfloat16)
    feed = product(activated, feed_down) + rows[15]
    result = third + table[5] * feed
    saved = (
        entered,
        packed,
        spatial_sum,
        attended,
        spatial,
        first,
        temporal_proj,
        temporal_att,
        temporal,
        second,
        query_text,
        keyval,
        cross_sum,
        cross_att,
        third,
        normed,
        hidden,
        activated,
        feed,
    )
    return (result.reshape(FRAMES, PATCH, width), saved)


def clip_backward(weights, totals, saved, block, words, table_in, length, kind, count, upstream):
    (
        spatial_in,
        spatial_out,
        temporal_in,
        temporal_out,
        cross_query,
        cross_keyval,
        cross_out,
        feed_up,
        feed_down,
        vectors,
        feed_bias,
    ) = weights
    (
        entered,
        packed,
        spatial_sum,
        attended,
        spatial,
        first,
        temporal_proj,
        temporal_att,
        temporal,
        second,
        query_text,
        keyval,
        cross_sum,
        cross_att,
        third,
        normed,
        hidden,
        activated,
        feed,
    ) = saved
    tokens = FRAMES * PATCH
    width = HEADS * HEAD
    table = vectors.astype(jnp.float32)[0:6] + table_in
    flat = block.reshape(tokens, width)
    upstream = upstream.reshape(tokens, width)
    d_feed = (table[5] * upstream).astype(jnp.bfloat16)
    grad_down = transposed(activated, d_feed)
    gate_b = jnp.sum(upstream * feed, axis=0)
    _, gelu_pull = jax.vjp(partial(jax.nn.gelu, approximate=True), hidden)
    d_hidden = gelu_pull(against(d_feed, feed_down))[0].astype(jnp.bfloat16)
    grad_up = transposed(normed, d_hidden)
    _, norm_pull = jax.vjp(modulate, third, table[3], table[4])
    d_third, shift_b, scale_b = norm_pull(against(d_hidden, feed_up))
    d_third = upstream + d_third
    d_cross = d_third.astype(jnp.bfloat16)
    grad_cross_out = transposed(cross_att, d_cross)
    d_cross_att = against(d_cross, cross_out).astype(jnp.bfloat16).reshape(tokens, HEADS, HEAD)
    text_mask = (jnp.arange(words.shape[0]) < length)[None, :]
    d_query, d_key, d_value = attend_backward(
        query_text, keyval[:, 0], keyval[:, 1], text_mask, cross_sum, d_cross_att
    )
    d_query = d_query.reshape(tokens, width)
    d_keyval = jnp.concatenate([d_key.reshape(-1, width), d_value.reshape(-1, width)], axis=1)
    grad_query = transposed(second.astype(jnp.bfloat16), d_query)
    grad_keyval = transposed(words.astype(jnp.bfloat16), d_keyval)
    d_text = against(d_keyval, cross_keyval)
    d_second = d_third + against(d_query, cross_query)
    d_temporal = (table[2] * d_second).astype(jnp.bfloat16)
    gate_a = jnp.sum(d_second * temporal, axis=0)
    grad_temporal_out = transposed(temporal_att, d_temporal)
    d_mixed = lax.optimization_barrier(
        against(d_temporal, temporal_out).astype(jnp.bfloat16)
    ).astype(jnp.float32)
    _, mix_pull = jax.vjp(partial(temporal_mix, pair=frame_pairs(kind, count)), temporal_proj)
    d_temporal_proj = mix_pull(d_mixed)[0].astype(jnp.bfloat16)
    grad_temporal_in = transposed(first.astype(jnp.bfloat16), d_temporal_proj)
    d_first = d_second + against(d_temporal_proj, temporal_in)
    d_spatial = (table[2] * d_first).astype(jnp.bfloat16)
    gate_a = gate_a + jnp.sum(d_first * spatial, axis=0)
    grad_spatial_out = transposed(attended, d_spatial)
    d_attended = against(d_spatial, spatial_out).astype(jnp.bfloat16).reshape(tokens, HEADS, HEAD)
    d_query_s, d_key_s, d_value_s = attend_backward(
        packed[:, 0],
        packed[:, 1],
        packed[:, 2],
        spatial_mask(kind, tokens),
        spatial_sum,
        d_attended,
    )
    d_packed = jnp.concatenate(
        [
            d_query_s.reshape(tokens, width),
            d_key_s.reshape(tokens, width),
            d_value_s.reshape(tokens, width),
        ],
        axis=1,
    )
    grad_spatial_in = transposed(entered, d_packed)
    _, input_pull = jax.vjp(modulate, flat, table[0], table[1])
    d_flat, shift_a, scale_a = input_pull(against(d_packed, spatial_in))
    d_input = d_first + d_flat
    packed_sum = column_sum(d_packed)
    temporal_sum = column_sum(d_temporal_proj)
    vector_grad = jnp.stack(
        [
            shift_a,
            scale_a,
            gate_a,
            shift_b,
            scale_b,
            gate_b,
            packed_sum[:width],
            packed_sum[2 * width :],
            column_sum(d_spatial),
            temporal_sum[:width],
            temporal_sum[2 * width :],
            column_sum(d_temporal),
            column_sum(d_query),
            column_sum(d_keyval)[width:],
            column_sum(d_cross),
            column_sum(d_feed),
        ]
    )
    terms = (
        grad_spatial_in,
        grad_spatial_out,
        grad_temporal_in,
        grad_temporal_out,
        grad_query,
        grad_keyval,
        grad_cross_out,
        grad_up,
        grad_down,
        vector_grad,
        column_sum(d_hidden),
    )
    updated = tuple((total + term for total, term in zip(totals, terms)))
    return (updated, d_input.reshape(FRAMES, PATCH, width), d_text)


def local(
    block_input,
    text,
    modulation,
    text_lengths,
    bucket,
    frames,
    cotangent,
    spatialqkv,
    spatialout,
    temporalqkv,
    temporalout,
    crossquery,
    crosskeyval,
    crossout,
    feedup,
    feeddown,
    vectors,
    feedbias,
):
    low_shards = tuple(
        (
            piece.astype(jnp.bfloat16)
            for piece in (
                spatialqkv,
                spatialout,
                temporalqkv,
                temporalout,
                crossquery,
                crosskeyval,
                crossout,
                feedup,
                feeddown,
                vectors,
                feedbias,
            )
        )
    )
    gathered = collect(low_shards)

    def forward_step(carry, items):
        block, words, table_in, length, kind, count = items
        result, saved = clip_forward(gathered, block, words, table_in, length, kind, count)
        return (carry, (result, saved))

    _, (block_output, stash) = lax.scan(
        forward_step, jnp.int32(0), (block_input, text, modulation, text_lengths, bucket, frames)
    )
    back_weights = recollect(low_shards)
    zeros = tuple((jnp.zeros(piece.shape, jnp.float32) for piece in back_weights))

    def backward_step(totals, items):
        saved, block, words, table_in, length, kind, count, upstream = items
        totals, d_input, d_text = clip_backward(
            back_weights, totals, saved, block, words, table_in, length, kind, count, upstream
        )
        return (totals, (d_input, d_text))

    totals, (input_grad, text_grad) = lax.scan(
        backward_step,
        zeros,
        (stash, block_input, text, modulation, text_lengths, bucket, frames, cotangent),
    )
    return (block_output, input_grad, text_grad) + tuple(spread(totals))


def solution(mesh):
    return jax.shard_map(
        local,
        mesh=mesh,
        in_specs=(
            P(("wide", "narrow"), None, None, None),
            P(("wide", "narrow"), None, None),
            P(("wide", "narrow"), None, None),
            P(("wide", "narrow")),
            P(("wide", "narrow")),
            P(("wide", "narrow")),
            P(("wide", "narrow"), None, None, None),
            P("narrow", "wide"),
            P("narrow", "wide"),
            P("narrow", "wide"),
            P("narrow", "wide"),
            P("narrow", "wide"),
            P("narrow", "wide"),
            P("narrow", "wide"),
            P("narrow", "wide"),
            P("narrow", "wide"),
            P("narrow", "wide"),
            P(("wide", "narrow")),
        ),
        out_specs=(
            P(("wide", "narrow"), None, None, None),
            P(("wide", "narrow"), None, None, None),
            P(("wide", "narrow"), None, None),
            P("narrow", "wide"),
            P("narrow", "wide"),
            P("narrow", "wide"),
            P("narrow", "wide"),
            P("narrow", "wide"),
            P("narrow", "wide"),
            P("narrow", "wide"),
            P("narrow", "wide"),
            P("narrow", "wide"),
            P("narrow", "wide"),
            P(("wide", "narrow")),
        ),
        check_vma=False,
    )
```

profile of v0, /device:TPU:0, one launch (start us, length us, event | category | flops | bytes accessed | tf_op | source)
XLA Modules:
  0.0 1802.6 jit_solution(10886449221062609034)
XLA Ops:
  89.1 22.4 %all-gather = bf16[16,72,16]{1,2,0:T(8,128)(2,1)S(1)} all-gather(bf16[1,72,16]{1,2,0:T(8,128)(2,1)S(1)} %bitcast.299), channel_id=1, replica_groups=mesh['wide'=16,'narrow'=2] {'wide'}, dimensions={0}, use_global_device_ids=true | all-gather | bytes 39168 | tf_op jit(solution)/shard_map/all_gather | solution.py:135
  124.5 60.1 %all-reduce.5 = bf16[4608]{0:T(1024)(128)(2,1)S(1)} all-reduce(bf16[4608]{0:T(1024)(128)(2,1)S(1)} %dynamic-update-slice.1), channel_id=1, replica_groups=mesh['wide'=16,'narrow'=2] {'wide'}, use_global_device_ids=true, to_apply=%add.5 | all-reduce | flops 4608 | bytes 18432
  245.0 22.2 %all-gather.23.cloned.1.call-done = bf16[1152,3456]{0,1:T(8,128)(2,1)} async-done(((bf16[1152,216]{0,1:T(8,128)(2,1)}), bf16[1152,3456]{0,1:T(8,128)(2,1)}) %all-gather.23.cloned.1.call-update) | async-done | bytes 7962640 | tf_op jit(solution)/shard_map/all_gather | solution.py:128
  296.9 41.7 %fusion.86 = (f32[256,16,2]{2,1,0:T(8,128)S(1)}, f32[256,16,2,2]{2,3,1,0:T(2,128)S(1)}) fusion(f32[2,256,16,72]{3,2,1,0:T(8,128)} %reshape.495, f32[2,256,16,72]{3,2,1,0:T(8,128)} %reshape.494, pred[2,2]{0,1:T(4,128)(4,1)S(1)} %compare_or_fusion), kind=kOutput, calls=%fused_computation.214 | convolution fusion | flops 14196736 | bytes 4816900 | tf_op jit(solution)/shard_map/while/body/eval_jaxpr/rphe,sphe->phrs/dot_general | solution.py:37
  346.6 16.2 convert_reduce_fusion
  364.9 35.7 %fusion.24 = bf16[2,256,16,72]{3,0,2,1:T(2,128)(2,1)} fusion(f32[256,16,2,2]{2,3,1,0:T(2,128)S(1)} %get-tuple-element.277, f32[2,256,16,72]{3,2,1,0:T(8,128)S(1)} %copy-done.48), kind=kOutput, calls=%fused_computation.71 | convolution fusion | flops 14745600 | bytes 3604480 | tf_op jit(solution)/shard_map/while/body/eval_jaxpr/phrs,sphe->rphe/dot_general | solution.py:41
  437.1 53.7 %all-gather.33.cloned.1.call-done = bf16[1152,4608]{0,1:T(8,128)(2,1)} async-done(((bf16[1152,288]{0,1:T(8,128)(2,1)}), bf16[1152,4608]{0,1:T(8,128)(2,1)}) %all-gather.33.cloned.1.call-update) | async-done | bytes 10616848 | tf_op jit(solution)/shard_map/all_gather | solution.py:133
  490.8 13.3 fusion.69
  504.1 75.6 %all-gather.35.cloned.1.call-done = bf16[4608,1152]{0,1:T(8,128)(2,1)} async-done(((bf16[4608,72]{0,1:T(8,128)(2,1)}), bf16[4608,1152]{0,1:T(8,128)(2,1)}) %all-gather.35.cloned.1.call-update) | async-done | bytes 10616848 | tf_op jit(solution)/shard_map/all_gather | solution.py:134
  579.7 16.3 fusion.71
  604.6 16.6 fusion.79
  656.8 17.4 convolution_bitcast_fusion.2
  674.2 28.2 %multiply_reduce_fusion.1 = (f32[256,16,2]{2,1,0:T(8,128)}, f32[256,16,2,2]{2,3,1,0:T(2,128)}) fusion(f32[256,16,2]{2,1,0:T(8,128)} %multiply_divide_fusion, f32[256,16,2,2]{2,3,1,0:T(2,128)S(1)} %copy-done.5, f32[256,16,2]{2,1,0:T(8,128)} %copy-done.18, bf16[256,16,72,2]{2,3,1,0:T(2,128)(2,1)} %copy.115, f32[2,256,16,72]{3,2,1,0:T(8,128)} %reshape.493), kind=kOutput, calls=%fused_computation.37 | convolution fusion | flops 14213120 | bytes 3768320 | tf_op jit(solution)/shard_map/while/body/eval_jaxpr/transpose(jvp(phrs,sphe->rphe))/dot_general | solution.py:41
  705.2 15.8 fusion.78
  723.9 33.9 %convolution_bitcast_fusion.1 = f32[2,256,16,72]{3,0,2,1:T(2,128)} fusion(f32[2,256,16,72]{3,2,1,0:T(8,128)S(1)} %copy-done.47, f32[256,16,2,2]{2,3,1,0:T(2,128)S(1)} %get-tuple-element.269, pred[256,16,2,2]{2,3,1,0:T(4,128)(4,1)S(1)} %copy-done.58, pred[2,2]{0,1:T(4,128)(4,1)S(1)} %copy-done.122, f32[256,16,2]{2,1,0:T(8,128)S(1)} %negate_divide_fusion), kind=kOutput, calls=%fused_computation.47 | convolution fusion | flops 14221312 | bytes 4833284 | tf_op jit(solution)/shard_map/while/body/eval_jaxpr/transpose(jvp(rphe,sphe->phrs))/dot_general | solution.py:37
  757.8 39.4 %convolution_bitcast_fusion = f32[2,256,16,72]{3,0,2,1:T(2,128)} fusion(f32[2,256,16,72]{3,2,1,0:T(8,128)S(1)} %copy-done.46, f32[256,16,2,2]{2,3,1,0:T(2,128)S(1)} %get-tuple-element.269, pred[256,16,2,2]{2,3,1,0:T(4,128)(4,1)S(1)} %copy-done.58, pred[2,2]{0,1:T(4,128)(4,1)S(1)} %copy-done.122, f32[256,16,2]{2,1,0:T(8,128)S(1)} %negate_divide_fusion), kind=kOutput, calls=%fused_computation.46 | convolution fusion | flops 14221312 | bytes 4833284 | tf_op jit(solution)/shard_map/while/body/eval_jaxpr/transpose(jvp(rphe,sphe->phrs))/dot_general | solution.py:37
  834.7 11.6 fusion.76
  888.8 13.4 multiply_reduce_fusion
  902.1 11.8 multiply_convert_fusion
  950.9 12.6 convolution_convert_fusion.1
  966.1 11.0 convolution_convert_fusion
  981.1 62.1 %reduce-scatter.80.cloned.1.call-done = bf16[1152,72]{0,1:T(8,128)(2,1)} async-done(((bf16[1152,1152]{0,1:T(8,128)(2,1)}), bf16[1152,72]{0,1:T(8,128)(2,1)}) %reduce-scatter.80.cloned.1.call-update) | async-done | bytes 165904
  1045.1 63.7 %reduce-scatter.78.cloned.1.call-done = bf16[1152,72]{0,1:T(8,128)(2,1)} async-done(((bf16[1152,1152]{0,1:T(8,128)(2,1)}), bf16[1152,72]{0,1:T(8,128)(2,1)}) %reduce-scatter.78.cloned.1.call-update) | async-done | bytes 165904
  1110.7 79.0 %reduce-scatter.48.cloned.1.call-done = bf16[1152,144]{0,1:T(8,128)(2,1)} async-done(((bf16[1152,2304]{0,1:T(8,128)(2,1)}), bf16[1152,144]{0,1:T(8,128)(2,1)}) %reduce-scatter.48.cloned.1.call-update) | async-done | bytes 331792 | tf_op jit(solution)/shard_map/reduce_scatter | solution.py:186
  1191.8 99.9 %reduce-scatter.72.cloned.1.call-done = bf16[1152,216]{0,1:T(8,128)(2,1)} async-done(((bf16[1152,3456]{0,1:T(8,128)(2,1)}), bf16[1152,216]{0,1:T(8,128)(2,1)}) %reduce-scatter.72.cloned.1.call-update) | async-done | bytes 497680
  1297.9 96.5 %reduce-scatter.76.cloned.1.call-done = bf16[1152,216]{0,1:T(8,128)(2,1)} async-done(((bf16[1152,3456]{0,1:T(8,128)(2,1)}), bf16[1152,216]{0,1:T(8,128)(2,1)}) %reduce-scatter.76.cloned.1.call-update) | async-done | bytes 497680
  1409.6 109.0 %reduce-scatter.50.cloned.1.call-done = bf16[1152,288]{0,1:T(8,128)(2,1)} async-done(((bf16[1152,4608]{0,1:T(8,128)(2,1)}), bf16[1152,288]{0,1:T(8,128)(2,1)}) %reduce-scatter.50.cloned.1.call-update) | async-done | bytes 663568 | tf_op jit(solution)/shard_map/reduce_scatter | solution.py:192
  1529.5 113.4 %reduce-scatter.52.cloned.1.call-done = bf16[4608,72]{0,1:T(8,128)(2,1)} async-done(((bf16[4608,1152]{0,1:T(8,128)(2,1)}), bf16[4608,72]{0,1:T(8,128)(2,1)}) %reduce-scatter.52.cloned.1.call-update) | async-done | bytes 663568 | tf_op jit(solution)/shard_map/reduce_scatter | solution.py:195
  1651.5 60.3 %all-reduce.16 = (bf16[16,1152]{1,0:T(8,128)(2,1)S(1)}, bf16[4608]{0:T(1024)(128)(2,1)S(1)}) all-reduce(bf16[16,1152]{1,0:T(8,128)(2,1)S(1)} %stack.85, bf16[4608]{0:T(1024)(128)(2,1)S(1)} %copy-done.97), channel_id=20, replica_groups=mesh['wide'=16,'narrow'=2] {'wide'}, use_global_device_ids=true, to_apply=%region_52.53.clone | all-reduce | flops 23040 | bytes 92160
  1738.3 16.2 reduce-scatter.60.cloned.1.call-done
  1756.6 18.7 %reduce-scatter.70.cloned.1.call-done = bf16[576,288]{1,0:T(8,128)(2,1)} async-done(((bf16[1152,288]{1,0:T(8,128)(2,1)}), bf16[576,288]{1,0:T(8,128)(2,1)}) %reduce-scatter.70.cloned.1.call-update) | async-done | bytes 331792
  1777.4 16.2 reduce-scatter.54.cloned.1.call-done
  (509 shorter events, 476.6 us)
Async XLA Ops:
  7.2 181.3 %all-gather.27.cloned.1.call-start = ((), (), s32[]{:S(2)}) async-start(), calls=%async_computation.22 | async-start | bytes 5640192 | tf_op jit(solution)/shard_map/all_gather | solution.py:131
  17.9 176.2 %all-gather.19.cloned.1.call-start = ((), (), s32[]{:S(2)}) async-start(), calls=%async_computation.18 | async-start | bytes 8460288 | tf_op jit(solution)/shard_map/all_gather | solution.py:126
  28.2 211.0 %all-gather.21.cloned.1.call-start = ((), (), s32[]{:S(2)}) async-start(), calls=%async_computation.19 | async-start | bytes 2820096 | tf_op jit(solution)/shard_map/all_gather | solution.py:127
  34.5 232.7 %all-gather.23.cloned.1.call-start = ((), (), s32[]{:S(2)}) async-start(), calls=%async_computation.20 | async-start | bytes 8460288 | tf_op jit(solution)/shard_map/all_gather | solution.py:128
  43.6 367.0 %all-gather.25.cloned.1.call-start = ((), (), s32[]{:S(2)}) async-start(), calls=%async_computation.21 | async-start | bytes 2820096 | tf_op jit(solution)/shard_map/all_gather | solution.py:129
  50.0 367.7 %all-gather.29.cloned.1.call-start = ((), (), s32[]{:S(2)}) async-start(), calls=%async_computation.23 | async-start | bytes 2820096 | tf_op jit(solution)/shard_map/all_gather | solution.py:130
  57.2 371.0 %all-gather.31.cloned.1.call-start = ((), (), s32[]{:S(2)}) async-start(), calls=%async_computation.24 | async-start | bytes 2820096 | tf_op jit(solution)/shard_map/all_gather | solution.py:132
  64.5 426.3 %all-gather.33.cloned.1.call-start = ((), (), s32[]{:S(2)}) async-start(), calls=%async_computation.25 | async-start | bytes 11280384 | tf_op jit(solution)/shard_map/all_gather | solution.py:133
  76.4 503.3 %all-gather.35.cloned.1.call-start = ((), (), s32[]{:S(2)}) async-start(), calls=%async_computation.26 | async-start | bytes 11280384 | tf_op jit(solution)/shard_map/all_gather | solution.py:134
  84.6 892.6 %reduce-scatter.74.cloned.1.call-start = ((), (), s32[]{:S(2)}) async-start(), calls=%async_computation.40 | async-start | bytes 2820096
  115.9 181.1 %copy-start.121 = (pred[2,2]{0,1:T(4,128)(4,1)}, pred[2,2]{0,1:T(4,128)(4,1)S(1)}, u32[]{:S(2)}) copy-start(pred[2,2]{0,1:T(4,128)(4,1)S(1)} %compare_or_fusion) | copy-start | bytes 16
  638.4 196.3 %copy-start.14 = (f32[512,1152]{1,0:T(8,128)}, f32[512,1152]{1,0:T(8,128)S(1)}, u32[]{:S(2)}) copy-start(f32[512,1152]{1,0:T(8,128)S(1)} %get-tuple-element.359) | copy-start | bytes 7077892
  850.7 128.5 %reduce-scatter.82.cloned.1.call-start = ((), (), s32[]{:S(2)}) async-start(), calls=%async_computation.44 | async-start | bytes 2820096
  856.9 186.3 %reduce-scatter.80.cloned.1.call-start = ((), (), s32[]{:S(2)}) async-start(), calls=%async_computation.43 | async-start | bytes 2820096
  863.2 245.6 %reduce-scatter.78.cloned.1.call-start = ((), (), s32[]{:S(2)}) async-start(), calls=%async_computation.42 | async-start | bytes 2820096
  868.2 321.5 %reduce-scatter.48.cloned.1.call-start = ((), (), s32[]{:S(2)}) async-start(), calls=%async_computation.27 | async-start | bytes 5640192 | tf_op jit(solution)/shard_map/reduce_scatter | solution.py:186
  879.4 412.3 %reduce-scatter.72.cloned.1.call-start = ((), (), s32[]{:S(2)}) async-start(), calls=%async_computation.39 | async-start | bytes 8460288
  938.9 455.5 %reduce-scatter.76.cloned.1.call-start = ((), (), s32[]{:S(2)}) async-start(), calls=%async_computation.41 | async-start | bytes 8460288
  949.2 569.4 %reduce-scatter.50.cloned.1.call-start = ((), (), s32[]{:S(2)}) async-start(), calls=%async_computation.28 | async-start | bytes 11280384 | tf_op jit(solution)/shard_map/reduce_scatter | solution.py:192
  963.5 679.4 %reduce-scatter.52.cloned.1.call-start = ((), (), s32[]{:S(2)}) async-start(), calls=%async_computation.29 | async-start | bytes 11280384 | tf_op jit(solution)/shard_map/reduce_scatter | solution.py:195
  977.2 745.3 %reduce-scatter.58.cloned.1.call-start = ((), (), s32[]{:S(2)}) async-start(), calls=%async_computation.32 | async-start | bytes 442368
  979.1 745.2 %reduce-scatter.68.cloned.1.call-start = ((), (), s32[]{:S(2)}) async-start(), calls=%async_computation.37 | async-start | bytes 442368
  981.0 745.0 %reduce-scatter.64.cloned.1.call-start = ((), (), s32[]{:S(2)}) async-start(), calls=%async_computation.35 | async-start | bytes 442368
  1045.0 682.7 %reduce-scatter.62.cloned.1.call-start = ((), (), s32[]{:S(2)}) async-start(), calls=%async_computation.34 | async-start | bytes 442368
  1110.6 285.9 %copy-start.3 = (f32[1,2,256,1152]{3,2,1,0:T(8,128)S(1)}, f32[1,2,256,1152]{3,2,1,0:T(8,128)}, u32[]{:S(2)}) copy-start(f32[1,2,256,1152]{3,2,1,0:T(8,128)} %param.18) | copy-start | bytes 7077892
  1110.6 285.9 %copy-start.25 = (bf16[16,72,512]{2,1,0:T(8,128)(2,1)S(1)}, bf16[16,72,512]{2,1,0:T(8,128)(2,1)}, u32[]{:S(2)}) copy-start(bf16[16,72,512]{2,1,0:T(8,128)(2,1)} %copy-done.24) | copy-start | bytes 3538948
  1110.7 285.9 %copy-start.81 = (f32[1152]{0:T(1024)S(1)}, f32[1152]{0:T(1024)}, u32[]{:S(2)}) copy-start(f32[1152]{0:T(1024)} %copy-done.80) | copy-start | bytes 13828
  1110.7 618.8 %reduce-scatter.66.cloned.1.call-start = ((), (), s32[]{:S(2)}) async-start(), calls=%async_computation.36 | async-start | bytes 884736
  1191.8 544.6 %reduce-scatter.56.cloned.1.call-start = ((), (), s32[]{:S(2)}) async-start(), calls=%async_computation.31 | async-start | bytes 884736
  1293.8 460.7 %reduce-scatter.60.cloned.1.call-start = ((), (), s32[]{:S(2)}) async-start(), calls=%async_computation.33 | async-start | bytes 884736
  1396.5 378.8 %reduce-scatter.70.cloned.1.call-start = ((), (), s32[]{:S(2)}) async-start(), calls=%async_computation.38 | async-start | bytes 1327104
  1521.0 272.7 %reduce-scatter.54.cloned.1.call-start = ((), (), s32[]{:S(2)}) async-start(), calls=%async_computation.30 | async-start | bytes 995328 | tf_op jit(solution)/shard_map/reduce_scatter | solution.py:230
  (119 other events, 1957.3 us)
Sparse Core Ops, SparseCore 0:
  18.0 57.8 all-gather.26
  78.6 70.9 all-gather.18
  152.3 41.7 all-gather.20
  196.7 70.4 all-gather.22
  269.8 41.8 all-gather.24
  314.2 41.8 all-gather.28
  358.8 41.8 all-gather.30
  403.6 87.1 all-gather.32
  493.1 86.5 all-gather.34
  850.8 61.0 reduce-scatter.73
  915.8 61.7 reduce-scatter.81
  981.4 61.7 reduce-scatter.79
  1047.1 61.6 reduce-scatter.77
  1112.7 76.9 reduce-scatter.47
  1193.6 98.0 reduce-scatter.71
  1295.7 98.6 reduce-scatter.75
  1398.3 120.3 reduce-scatter.49
  1522.6 120.2 reduce-scatter.51
  1645.7 11.7 reduce-scatter.57
  1659.6 12.0 reduce-scatter.67
  1673.9 12.1 reduce-scatter.63
  1688.3 12.1 reduce-scatter.61
  1702.8 15.5 reduce-scatter.65
  1721.0 15.2 reduce-scatter.55
  1739.2 15.3 reduce-scatter.59
  1756.7 18.5 reduce-scatter.69
  1777.4 16.1 reduce-scatter.53
where the time goes:
time: 1810 us; the launch traced here: 1800 us
  waiting for transfers between devices  832 us (46%)
  matrix products  457 us (25%)
  blocking collectives  222 us (12%)
  local copies, waits for them, and re-layouts  165 us (9%)
  other arithmetic  103 us (6%)
  between operations  22.1 us (1%)
    unnamed x41, waiting for transfers between devices  363 us
    unnamed x4, blocking collectives  130 us
    dot_general x3, matrix products, temporal_mix(): jnp.einsum('rphe,sphe->phrs', split[0], split[1], precision=lax.Precision...  115 us
    reduce_scatter x1, waiting for transfers between devices, spread(): lax.psum_scatter(grads[8].astype(jnp.bfloat16), 'wide', scatter_dimension...  113 us
    reduce_scatter x1, waiting for transfers between devices, spread(): lax.psum_scatter(grads[7].astype(jnp.bfloat16), 'wide', scatter_dimension...  109 us
    dot_general x3, matrix products, temporal_mix(): jnp.einsum('phrs,sphe->rphe', softmax_rows(scores), split[2], precision=l...  81.3 us
    reduce_scatter x1, waiting for transfers between devices, spread(): lax.psum_scatter(grads[5].astype(jnp.bfloat16), 'wide', scatter_dimension...  79 us
    all_gather x1, waiting for transfers between devices, collect(): lax.all_gather(part[8], 'wide', axis=1, tiled=True)  75.6 us
  transfers between devices with their start and end apart: 27, of which 14 were waited for; matrix products, arithmetic and copies ran while one was open for 24% of the time, Pallas kernels for 0%

commit v1 on v0

v1 whole, which is shorter than its diff:
```python
from functools import partial

import jax
import jax.numpy as jnp
from jax import lax
from jax.experimental import pallas as pl
from jax.experimental.pallas import tpu as pltpu
from jax.sharding import PartitionSpec as P

HEADS = 16
HEAD = 72
PATCH = 256
FRAMES = 2


def layer_norm(value):
    mean = jnp.mean(value, axis=-1, keepdims=True)
    centered = value - mean
    variance = jnp.mean(centered * centered, axis=-1, keepdims=True)
    return centered * lax.rsqrt(variance + 1e-06)


def modulate(value, shift, scale):
    return layer_norm(value) * (1.0 + scale) + shift


def softmax_rows(scores):
    top = jnp.max(scores, axis=-1, keepdims=True)
    powers = jnp.exp(scores - top)
    return powers / jnp.sum(powers, axis=-1, keepdims=True)


def head_sum(value, ones):
    high = value.astype(jnp.bfloat16)
    rest = value - high.astype(jnp.float32)
    middle = rest.astype(jnp.bfloat16)
    small = (rest - middle.astype(jnp.float32)).astype(jnp.bfloat16)

    def part(piece):
        return jnp.dot(piece, ones, preferred_element_type=jnp.float32)

    return part(high) + (part(middle) + part(small))


def head_spread(value, ones):
    high = value.astype(jnp.bfloat16)
    rest = value - high.astype(jnp.float32)
    middle = rest.astype(jnp.bfloat16)
    small = (rest - middle.astype(jnp.float32)).astype(jnp.bfloat16)

    def part(piece):
        return lax.dot_general(
            piece, ones, (((1,), (1,)), ((), ())), preferred_element_type=jnp.float32
        )

    return part(high) + (part(middle) + part(small))


def temporal_probs(pair_ref, proj_ref, ones):
    width = HEADS * HEAD
    query = [proj_ref[r, :, 0:width] for r in range(FRAMES)]
    key = [proj_ref[r, :, width : 2 * width] for r in range(FRAMES)]
    both = pair_ref[0] > 0
    probs = []
    for r in range(FRAMES):
        scores = [head_sum(query[r] * key[s], ones) * HEAD ** (-0.5) for s in range(FRAMES)]
        scores = [
            scores[s] if s == r else jnp.where(both, scores[s], -1000000000.0)
            for s in range(FRAMES)
        ]
        top = scores[0]
        for s in range(1, FRAMES):
            top = jnp.maximum(top, scores[s])
        powers = [jnp.exp(score - top) for score in scores]
        total = powers[0]
        for s in range(1, FRAMES):
            total = total + powers[s]
        probs.append([power / total for power in powers])
    return query, key, probs


def temporal_forward_kernel(pair_ref, proj_ref, ones_ref, out_ref):
    width = HEADS * HEAD
    ones = ones_ref[...]
    _, _, probs = temporal_probs(pair_ref, proj_ref, ones)
    value = [proj_ref[s, :, 2 * width :] for s in range(FRAMES)]
    for r in range(FRAMES):
        mixed = head_spread(probs[r][0], ones) * value[0]
        for s in range(1, FRAMES):
            mixed = mixed + head_spread(probs[r][s], ones) * value[s]
        out_ref[r] = mixed.astype(out_ref.dtype)


def temporal_backward_kernel(pair_ref, proj_ref, grad_ref, ones_ref, out_ref):
    width = HEADS * HEAD
    ones = ones_ref[...]
    query, key, probs = temporal_probs(pair_ref, proj_ref, ones)
    value = [proj_ref[s, :, 2 * width :] for s in range(FRAMES)]
    grad = [grad_ref[r].astype(jnp.float32) for r in range(FRAMES)]
    slope = []
    for r in range(FRAMES):
        through = [head_sum(grad[r] * value[s], ones) for s in range(FRAMES)]
        inner = probs[r][0] * through[0]
        for s in range(1, FRAMES):
            inner = inner + probs[r][s] * through[s]
        slope.append(
            [
                head_spread(probs[r][s] * (through[s] - inner) * HEAD ** (-0.5), ones)
                for s in range(FRAMES)
            ]
        )
    for r in range(FRAMES):
        d_query = slope[r][0] * key[0]
        for s in range(1, FRAMES):
            d_query = d_query + slope[r][s] * key[s]
        out_ref[r, :, 0:width] = d_query.astype(out_ref.dtype)
    for s in range(FRAMES):
        d_key = slope[0][s] * query[0]
        d_value = head_spread(probs[0][s], ones) * grad[0]
        for r in range(1, FRAMES):
            d_key = d_key + slope[r][s] * query[r]
            d_value = d_value + head_spread(probs[r][s], ones) * grad[r]
        out_ref[s, :, width : 2 * width] = d_key.astype(out_ref.dtype)
        out_ref[s, :, 2 * width :] = d_value.astype(out_ref.dtype)


def head_ones():
    lane = jnp.arange(HEADS * HEAD, dtype=jnp.int32)[:, None] // HEAD
    return (lane == jnp.arange(128, dtype=jnp.int32)[None, :]).astype(jnp.bfloat16)


TEMPORAL_ROWS = 64


def temporal_call(kernel, pair, arrays, columns):
    rows = arrays[0].shape[1]
    step = min(TEMPORAL_ROWS, rows)
    ones = head_ones()
    return pl.pallas_call(
        kernel,
        grid=(rows // step,),
        in_specs=[pl.BlockSpec(memory_space=pltpu.SMEM)]
        + [
            pl.BlockSpec((FRAMES, step, array.shape[2]), lambda i: (0, i, 0)) for array in arrays
        ]
        + [pl.BlockSpec(ones.shape, lambda i: (0, 0))],
        out_specs=pl.BlockSpec((FRAMES, step, columns), lambda i: (0, i, 0)),
        out_shape=jax.ShapeDtypeStruct((FRAMES, rows, columns), jnp.bfloat16),
        compiler_params=pltpu.CompilerParams(vmem_limit_bytes=48 * 1024 * 1024),
        cost_estimate=pl.CostEstimate(
            flops=20 * FRAMES * rows * columns * 128, bytes_accessed=16000000, transcendentals=0
        ),
    )(pair, *arrays, ones)


def temporal_mix(projected, pair):
    width = HEADS * HEAD
    shaped = projected.reshape(FRAMES, -1, 3 * width)
    return temporal_call(temporal_forward_kernel, pair, (shaped,), width).reshape(-1, width)


def temporal_pull(projected, grad, pair):
    width = HEADS * HEAD
    shaped = projected.reshape(FRAMES, -1, 3 * width)
    grad = grad.reshape(FRAMES, -1, width)
    return temporal_call(temporal_backward_kernel, pair, (shaped, grad), 3 * width).reshape(
        -1, 3 * width
    )


def product(left, right):
    return jnp.dot(left, right, preferred_element_type=jnp.float32)


def transposed(left, right):
    return lax.dot_general(
        left, right, (((0,), (0,)), ((), ())), preferred_element_type=jnp.float32
    )


def against(left, right):
    return lax.dot_general(
        left, right, (((1,), (1,)), ((), ())), preferred_element_type=jnp.float32
    )


def gradient(left, right):
    return transposed(right, left).astype(jnp.bfloat16)


def column_sum(value):
    return jnp.sum(value, axis=0, dtype=jnp.float32)


def spatial_mask(kind, tokens):
    segment = jnp.where(kind == 0, jnp.arange(tokens) // PATCH, 0)
    return segment[:, None] == segment[None, :]


def frame_pairs(kind, count):
    return ((kind == 0) & (count == 2)).astype(jnp.int32).reshape(1)


def masked_scores(queries, keys, allowed):
    scores = jnp.einsum(
        "lhe,mhe->hlm", queries, keys, preferred_element_type=jnp.float32
    ) * HEAD ** (-0.5)
    return jnp.where(allowed[None], scores, -1000000000.0)


def attend_forward(queries, keys, values, allowed):
    scores = masked_scores(queries, keys, allowed)
    top = jnp.max(scores, axis=-1, keepdims=True)
    powers = jnp.exp(scores - top)
    total = jnp.sum(powers, axis=-1, keepdims=True)
    probs = (powers / total).astype(jnp.bfloat16)
    mixed = jnp.einsum("hlm,mhe->lhe", probs, values, preferred_element_type=jnp.float32)
    return (mixed, top + jnp.log(total))


def attend_backward(queries, keys, values, allowed, logsum, upstream):
    scale = HEAD ** (-0.5)
    probs = jnp.exp(masked_scores(queries, keys, allowed) - logsum)
    through = jnp.einsum("lhe,mhe->hlm", upstream, values, preferred_element_type=jnp.float32)
    inner = jnp.sum(probs * through, axis=-1, keepdims=True)
    slopes = (probs * (through - inner)).astype(jnp.bfloat16)
    d_queries = (
        jnp.einsum("hlm,mhe->lhe", slopes, keys, preferred_element_type=jnp.float32) * scale
    ).astype(jnp.bfloat16)
    d_keys = (
        jnp.einsum("hlm,lhe->mhe", slopes, queries, preferred_element_type=jnp.float32) * scale
    ).astype(jnp.bfloat16)
    d_values = jnp.einsum(
        "hlm,lhe->mhe", probs.astype(jnp.bfloat16), upstream, preferred_element_type=jnp.float32
    ).astype(jnp.bfloat16)
    return (d_queries, d_keys, d_values)


GROUPS = ((0, 1), (2, 3, 4, 5, 6), (7, 8))
BACK_GROUPS = ((8,), (7,), (4, 5, 6), (2, 3), (0, 1))


def to_rows(value, columns):
    flat = value.reshape(value.shape[:-1] + (-1,)) if value.ndim > 1 else value
    flat = value.reshape(-1)
    rows = -(-flat.shape[0] // (8 * columns)) * 8
    return jnp.pad(flat, (0, rows * columns - flat.shape[0])).reshape(rows, columns)


def as_rows(shard, columns):
    return shard.T.reshape(-1, columns)


def collect(shards):
    wide, narrow = lax.axis_size("wide"), lax.axis_size("narrow")
    columns = shards[0].shape[0]
    weights = [None] * 9
    for number, group in enumerate(GROUPS):
        pieces = [as_rows(shards[index], columns) for index in group]
        if number == 0:
            pieces += [to_rows(shards[9], columns), to_rows(shards[10], columns)]
        packed = jnp.concatenate(pieces, axis=0)
        whole = lax.all_gather(packed, ("wide", "narrow"), axis=0, tiled=True)
        whole = whole.reshape(wide, narrow, packed.shape[0], columns)
        start = 0
        for place, piece in enumerate(pieces):
            part = whole[:, :, start : start + piece.shape[0]]
            start += piece.shape[0]
            if place < len(group):
                index = group[place]
                own, depth = shards[index].shape[1], shards[index].shape[0]
                part = part.reshape(wide, narrow, own, depth // columns, columns)
                part = part.transpose(0, 2, 1, 3, 4)
                weights[index] = part.reshape(wide * own, narrow * depth)
            elif place == len(group):
                rows, own = shards[9].shape
                part = part.reshape(wide, narrow, -1)[:, :, : rows * own]
                part = part.reshape(wide, narrow, rows, own).transpose(1, 2, 0, 3)
                vectors = part.reshape(narrow * rows, wide * own)
            else:
                bias = part.reshape(wide * narrow, -1)[:, : shards[10].shape[0]].reshape(-1)
    return tuple(weights) + (vectors, bias)


def spread(grads, shards):
    wide, narrow = lax.axis_size("wide"), lax.axis_size("narrow")
    columns = shards[0].shape[0]
    result = [None] * 11
    for number, group in enumerate(BACK_GROUPS):
        pieces = []
        for index in group:
            depth, own = shards[index].shape
            part = grads[index].reshape(wide, own, narrow, depth // columns, columns)
            pieces.append(part.transpose(0, 2, 1, 3, 4).reshape(wide, narrow, -1, columns))
        if number == len(BACK_GROUPS) - 1:
            rows, own = shards[9].shape
            part = grads[9].astype(jnp.bfloat16).reshape(narrow, rows, wide, own)
            part = part.transpose(2, 0, 1, 3).reshape(wide * narrow, -1)
            pieces.append(jax.vmap(partial(to_rows, columns=columns))(part))
            part = grads[10].astype(jnp.bfloat16).reshape(wide * narrow, -1)
            pieces.append(jax.vmap(partial(to_rows, columns=columns))(part))
            pieces[-2:] = [
                piece.reshape(wide, narrow, -1, columns) for piece in pieces[-2:]
            ]
        packed = jnp.concatenate(pieces, axis=2)
        count = packed.shape[2]
        mine = lax.psum_scatter(
            packed.reshape(wide * narrow * count, columns),
            ("wide", "narrow"),
            scatter_dimension=0,
            tiled=True,
        ).astype(jnp.float32)
        start = 0
        for place, piece in enumerate(pieces):
            part = mine[start : start + piece.shape[2]]
            start += piece.shape[2]
            if place < len(group):
                depth, own = shards[group[place]].shape
                result[group[place]] = part.reshape(own, depth).T
            else:
                shard = shards[9 + place - len(group)]
                result[9 + place - len(group)] = part.reshape(-1)[: shard.size].reshape(
                    shard.shape
                )
    return tuple(result)


def clip_forward(weights, block, words, table_in, length, kind, count):
    (
        spatial_in,
        spatial_out,
        temporal_in,
        temporal_out,
        cross_query,
        cross_keyval,
        cross_out,
        feed_up,
        feed_down,
        vectors,
        feed_bias,
    ) = weights
    tokens = FRAMES * PATCH
    width = HEADS * HEAD
    rows = vectors.astype(jnp.float32)
    table = rows[0:6] + table_in
    blank = jnp.zeros((width,), jnp.float32)
    flat = block.reshape(tokens, width)
    entered = modulate(flat, table[0], table[1]).astype(jnp.bfloat16)
    packed = (
        (against(entered, spatial_in) + jnp.concatenate([rows[6], blank, rows[7]]))
        .astype(jnp.bfloat16)
        .reshape(tokens, 3, HEADS, HEAD)
    )
    mixed, spatial_sum = attend_forward(
        packed[:, 0], packed[:, 1], packed[:, 2], spatial_mask(kind, tokens)
    )
    attended = mixed.reshape(tokens, width).astype(jnp.bfloat16)
    spatial = against(attended, spatial_out) + rows[8]
    first = flat + table[2] * spatial
    temporal_proj = against(first.astype(jnp.bfloat16), temporal_in) + jnp.concatenate(
        [rows[9], blank, rows[10]]
    )
    temporal_att = temporal_mix(temporal_proj, frame_pairs(kind, count))
    temporal = against(temporal_att, temporal_out) + rows[11]
    second = first + table[2] * temporal
    query_text = (
        (against(second.astype(jnp.bfloat16), cross_query) + rows[12])
        .astype(jnp.bfloat16)
        .reshape(tokens, HEADS, HEAD)
    )
    keyval = (
        (against(words.astype(jnp.bfloat16), cross_keyval) + jnp.concatenate([blank, rows[13]]))
        .astype(jnp.bfloat16)
        .reshape(-1, 2, HEADS, HEAD)
    )
    text_mask = (jnp.arange(words.shape[0]) < length)[None, :]
    mixed, cross_sum = attend_forward(query_text, keyval[:, 0], keyval[:, 1], text_mask)
    cross_att = mixed.reshape(tokens, width).astype(jnp.bfloat16)
    third = second + (against(cross_att, cross_out) + rows[14])
    normed = modulate(third, table[3], table[4]).astype(jnp.bfloat16)
    hidden = against(normed, feed_up) + feed_bias.astype(jnp.float32)
    activated = jax.nn.gelu(hidden, approximate=True).astype(jnp.bfloat16)
    feed = against(activated, feed_down) + rows[15]
    result = third + table[5] * feed
    saved = (
        entered,
        packed,
        spatial_sum,
        attended,
        spatial,
        first,
        temporal_proj,
        temporal_att,
        temporal,
        second,
        query_text,
        keyval,
        cross_sum,
        cross_att,
        third,
        normed,
        hidden,
        activated,
        feed,
    )
    return (result.reshape(FRAMES, PATCH, width), saved)


def clip_backward(weights, saved, block, words, table_in, length, kind, count, upstream):
    (
        spatial_in,
        spatial_out,
        temporal_in,
        temporal_out,
        cross_query,
        cross_keyval,
        cross_out,
        feed_up,
        feed_down,
        vectors,
        feed_bias,
    ) = weights
    (
        entered,
        packed,
        spatial_sum,
        attended,
        spatial,
        first,
        temporal_proj,
        temporal_att,
        temporal,
        second,
        query_text,
        keyval,
        cross_sum,
        cross_att,
        third,
        normed,
        hidden,
        activated,
        feed,
    ) = saved
    tokens = FRAMES * PATCH
    width = HEADS * HEAD
    table = vectors.astype(jnp.float32)[0:6] + table_in
    flat = block.reshape(tokens, width)
    upstream = upstream.reshape(tokens, width)
    d_feed = (table[5] * upstream).astype(jnp.bfloat16)
    grad_down = gradient(activated, d_feed)
    gate_b = jnp.sum(upstream * feed, axis=0)
    _, gelu_pull = jax.vjp(partial(jax.nn.gelu, approximate=True), hidden)
    d_hidden = gelu_pull(product(d_feed, feed_down))[0].astype(jnp.bfloat16)
    grad_up = gradient(normed, d_hidden)
    _, norm_pull = jax.vjp(modulate, third, table[3], table[4])
    d_third, shift_b, scale_b = norm_pull(product(d_hidden, feed_up))
    d_third = upstream + d_third
    d_cross = d_third.astype(jnp.bfloat16)
    grad_cross_out = gradient(cross_att, d_cross)
    d_cross_att = product(d_cross, cross_out).astype(jnp.bfloat16).reshape(tokens, HEADS, HEAD)
    text_mask = (jnp.arange(words.shape[0]) < length)[None, :]
    d_query, d_key, d_value = attend_backward(
        query_text, keyval[:, 0], keyval[:, 1], text_mask, cross_sum, d_cross_att
    )
    d_query = d_query.reshape(tokens, width)
    d_keyval = jnp.concatenate([d_key.reshape(-1, width), d_value.reshape(-1, width)], axis=1)
    grad_query = gradient(second.astype(jnp.bfloat16), d_query)
    grad_keyval = gradient(words.astype(jnp.bfloat16), d_keyval)
    d_text = product(d_keyval, cross_keyval)
    d_second = d_third + product(d_query, cross_query)
    d_temporal = (table[2] * d_second).astype(jnp.bfloat16)
    gate_a = jnp.sum(d_second * temporal, axis=0)
    grad_temporal_out = gradient(temporal_att, d_temporal)
    d_mixed = product(d_temporal, temporal_out).astype(jnp.bfloat16)
    d_temporal_proj = temporal_pull(temporal_proj, d_mixed, frame_pairs(kind, count))
    grad_temporal_in = gradient(first.astype(jnp.bfloat16), d_temporal_proj)
    d_first = d_second + product(d_temporal_proj, temporal_in)
    d_spatial = (table[2] * d_first).astype(jnp.bfloat16)
    gate_a = gate_a + jnp.sum(d_first * spatial, axis=0)
    grad_spatial_out = gradient(attended, d_spatial)
    d_attended = product(d_spatial, spatial_out).astype(jnp.bfloat16).reshape(tokens, HEADS, HEAD)
    d_query_s, d_key_s, d_value_s = attend_backward(
        packed[:, 0],
        packed[:, 1],
        packed[:, 2],
        spatial_mask(kind, tokens),
        spatial_sum,
        d_attended,
    )
    d_packed = jnp.concatenate(
        [
            d_query_s.reshape(tokens, width),
            d_key_s.reshape(tokens, width),
            d_value_s.reshape(tokens, width),
        ],
        axis=1,
    )
    grad_spatial_in = gradient(entered, d_packed)
    _, input_pull = jax.vjp(modulate, flat, table[0], table[1])
    d_flat, shift_a, scale_a = input_pull(product(d_packed, spatial_in))
    d_input = d_first + d_flat
    packed_sum = column_sum(d_packed)
    temporal_sum = column_sum(d_temporal_proj)
    vector_grad = jnp.stack(
        [
            shift_a,
            scale_a,
            gate_a,
            shift_b,
            scale_b,
            gate_b,
            packed_sum[:width],
            packed_sum[2 * width :],
            column_sum(d_spatial),
            temporal_sum[:width],
            temporal_sum[2 * width :],
            column_sum(d_temporal),
            column_sum(d_query),
            column_sum(d_keyval)[width:],
            column_sum(d_cross),
            column_sum(d_feed),
        ]
    )
    terms = (
        grad_spatial_in,
        grad_spatial_out,
        grad_temporal_in,
        grad_temporal_out,
        grad_query,
        grad_keyval,
        grad_cross_out,
        grad_up,
        grad_down,
        vector_grad,
        column_sum(d_hidden),
    )
    return (terms, d_input.reshape(FRAMES, PATCH, width), d_text)


def local(
    block_input,
    text,
    modulation,
    text_lengths,
    bucket,
    frames,
    cotangent,
    spatialqkv,
    spatialout,
    temporalqkv,
    temporalout,
    crossquery,
    crosskeyval,
    crossout,
    feedup,
    feeddown,
    vectors,
    feedbias,
):
    low_shards = tuple(
        (
            piece.astype(jnp.bfloat16)
            for piece in (
                spatialqkv,
                spatialout,
                temporalqkv,
                temporalout,
                crossquery,
                crosskeyval,
                crossout,
                feedup,
                feeddown,
                vectors,
                feedbias,
            )
        )
    )
    weights = collect(low_shards)
    count = block_input.shape[0]
    outputs, input_grads, text_grads, totals = [], [], [], None
    for sample in range(count):
        items = (
            block_input[sample],
            text[sample],
            modulation[sample],
            text_lengths[sample],
            bucket[sample],
            frames[sample],
        )
        result, saved = clip_forward(weights, *items)
        terms, d_input, d_text = clip_backward(weights, saved, *items, cotangent[sample])
        outputs.append(result)
        input_grads.append(d_input)
        text_grads.append(d_text)
        if totals is None:
            totals = terms
        else:
            totals = tuple(
                (total.astype(jnp.float32) + term).astype(term.dtype)
                for total, term in zip(totals, terms)
            )
    return (jnp.stack(outputs), jnp.stack(input_grads), jnp.stack(text_grads)) + spread(
        totals, low_shards
    )


def solution(mesh):
    return jax.shard_map(
        local,
        mesh=mesh,
        in_specs=(
            P(("wide", "narrow"), None, None, None),
            P(("wide", "narrow"), None, None),
            P(("wide", "narrow"), None, None),
            P(("wide", "narrow")),
            P(("wide", "narrow")),
            P(("wide", "narrow")),
            P(("wide", "narrow"), None, None, None),
            P("narrow", "wide"),
            P("narrow", "wide"),
            P("narrow", "wide"),
            P("narrow", "wide"),
            P("narrow", "wide"),
            P("narrow", "wide"),
            P("narrow", "wide"),
            P("narrow", "wide"),
            P("narrow", "wide"),
            P("narrow", "wide"),
            P(("wide", "narrow")),
        ),
        out_specs=(
            P(("wide", "narrow"), None, None, None),
            P(("wide", "narrow"), None, None, None),
            P(("wide", "narrow"), None, None),
            P("narrow", "wide"),
            P("narrow", "wide"),
            P("narrow", "wide"),
            P("narrow", "wide"),
            P("narrow", "wide"),
            P("narrow", "wide"),
            P("narrow", "wide"),
            P("narrow", "wide"),
            P("narrow", "wide"),
            P("narrow", "wide"),
            P(("wide", "narrow")),
        ),
        check_vma=False,
    )
```

time: 1810 us -> 1690 us (0.934)
  local copies, waits for them, and re-layouts: 165 us -> 551 us
  blocking collectives: 222 us -> 0 us
  matrix products: 457 us -> 245 us
  waiting for transfers between devices: 832 us -> 667 us
  other arithmetic: 103 us -> 171 us
  Pallas kernels: 0 us -> 28.9 us
    unnamed x41 -> x8, waiting for transfers between devices: 363 us -> 0.13 us
    reshape x4 -> x33, local copies, waits for them, and re-layouts: 22.3 us -> 260 us  [the longest x10 133 us: spread(): part = grads[index].reshape(wide, own, narrow, depth // columns, columns)]
    dot_general x6 -> x0, matrix products: 196 us -> none  [the longest x3 115 us: temporal_mix(): jnp.einsum('rphe,sphe->phrs', split[0], split[1], precision=lax.Precision...]
    unnamed x4 -> x0, blocking collectives: 130 us -> none
    concatenate x0 -> x6, other arithmetic: none -> 118 us  [the longest x3 116 us: spread(): packed = jnp.concatenate(pieces, axis=2)]
    all_gather x9 -> x3, waiting for transfers between devices: 152 us -> 256 us  [collect(): whole = lax.all_gather(packed, ('wide', 'narrow'), axis=0, tiled=True)]
    reduce_scatter x4 -> x5, waiting for transfers between devices: 318 us -> 412 us  [spread(): lax.psum_scatter(packed.reshape(wide * narrow * count, columns), ('wide',...]
    all_gather x11 -> x0, blocking collectives: 91.7 us -> none  [the longest x1 22.4 us: collect(): lax.all_gather(part[9], 'wide', axis=1, tiled=True)]
  transfers between devices with their start and end apart: 27 -> 8, of which waited for: 14 -> 5; matrix products, arithmetic and copies ran while one was open for 24% -> 34% of each run, Pallas kernels for 0% -> 1%
where the time goes in v1:
time: 1690 us; the launch traced here: 1680 us
  waiting for transfers between devices  667 us (39%)
  local copies, waits for them, and re-layouts  551 us (33%)
  matrix products  245 us (14%)
  other arithmetic  171 us (10%)
  Pallas kernels  28.9 us (2%)
  between operations  17.6 us (1%)
    reduce_scatter x5, waiting for transfers between devices, spread(): lax.psum_scatter(packed.reshape(wide * narrow * count, columns), ('wide',...  412 us
    all_gather x3, waiting for transfers between devices, collect(): whole = lax.all_gather(packed, ('wide', 'narrow'), axis=0, tiled=True)  256 us
    reshape x10, local copies, waits for them, and re-layouts, spread(): part = grads[index].reshape(wide, own, narrow, depth // columns, columns)  133 us
    concatenate x3, other arithmetic, spread(): packed = jnp.concatenate(pieces, axis=2)  116 us
    reshape x9, local copies, waits for them, and re-layouts, collect(): weights[index] = part.reshape(wide * own, narrow * depth)  114 us
    unnamed x221, local copies, waits for them, and re-layouts  81.6 us
    transpose x4, local copies, waits for them, and re-layouts, collect(): part = part.transpose(0, 2, 1, 3, 4)  68.7 us
    dot_general x9, matrix products, against(): lax.dot_general(left, right, (((1,), (1,)), ((), ())), preferred_element_...  64.9 us
  transfers between devices with their start and end apart: 8, of which 5 were waited for; matrix products, arithmetic and copies ran while one was open for 34% of the time, Pallas kernels for 1%

profile of v1, /device:TPU:0, one launch (start us, length us, event | category | flops | bytes accessed | tf_op | source)
XLA Modules:
  0.0 1680.5 jit_solution(6617781362956709535)
XLA Ops:
  22.4 87.1 %all-gather.4.cloned.1.call-done = bf16[9728,576]{1,0:T(8,128)(2,1)} async-done(((bf16[304,576]{1,0:T(8,128)(2,1)}), bf16[9728,576]{1,0:T(8,128)(2,1)}) %all-gather.4.cloned.1.call-update) | async-done | bytes 11206672 | tf_op jit(solution)/shard_map/all_gather | solution.py:263
  126.0 13.8 copy.161
  139.8 14.8 reshape.525
  217.2 40.7 %all-gather.6.cloned.1.call-done = bf16[18432,576]{1,0:T(8,128)(2,1)} async-done(((bf16[576,576]{1,0:T(8,128)(2,1)}), bf16[18432,576]{1,0:T(8,128)(2,1)}) %all-gather.6.cloned.1.call-update) | async-done | bytes 21233680 | tf_op jit(solution)/shard_map/all_gather | solution.py:263
  277.7 127.7 %all-gather.8.cloned.1.call-done = bf16[18432,576]{1,0:T(8,128)(2,1)} async-done(((bf16[576,576]{1,0:T(8,128)(2,1)}), bf16[18432,576]{1,0:T(8,128)(2,1)}) %all-gather.8.cloned.1.call-update) | async-done | bytes 21233680 | tf_op jit(solution)/shard_map/all_gather | solution.py:263
  405.5 13.0 slice_bitcast_fusion
  418.5 27.8 %copy.117 = bf16[16,288,2,1,576]{4,2,1,0,3:T(2,128)(2,1)} copy(bf16[16,288,2,1,576]{4,1,2,0,3:T(8,128)(2,1)S(1)} %get-tuple-element.50) | data formatting | bytes 21233664 | tf_op jit(solution)/shard_map/transpose | solution.py:273
  446.3 23.0 %reshape.549 = bf16[4608,1152]{1,0:T(8,128)(2,1)} reshape(bf16[16,288,2,1,576]{4,2,1,0,3:T(2,128)(2,1)} %copy.117) | data formatting | bytes 21233664 | tf_op jit(solution)/shard_map/reshape | solution.py:274
  469.4 20.5 %copy.162 = bf16[16,2,144,576]{3,1,2,0:T(2,128)(2,1)} copy(bf16[16,2,144,576]{3,2,1,0:T(8,128)(2,1)} %slice.239) | data formatting | bytes 10616832
  489.9 12.4 reshape.539
  509.0 13.9 copy.160
  522.9 14.8 reshape.533
  537.6 18.7 %copy_bitcast_fusion.4 = (bf16[16,72,2,1,576]{4,2,1,0,3:T(2,128)(2,1)}, bf16[16,72,2,1,576]{4,2,1,0,3:T(2,128)(2,1)}) fusion(bf16[16,2,72,576]{3,2,1,0:T(8,128)(2,1)} %get-tuple-element.52, bf16[16,2,72,576]{3,2,1,0:T(8,128)(2,1)} %get-tuple-element.53), kind=kLoop, calls=%fused_computation.66 | loop fusion | bytes 10616832 | tf_op jit(solution)/shard_map/transpose | solution.py:273
  582.6 18.4 %copy.118 = bf16[16,2,288,576]{3,0,2,1:T(8,128)(2,1)S(1)} copy(bf16[16,2,288,576]{3,2,1,0:T(8,128)(2,1)} %get-tuple-element.51) | data formatting | bytes 21233664 | tf_op jit(solution)/shard_map/slice | solution.py:267
  610.1 21.8 %reshape.552 = bf16[1152,4608]{1,0:T(8,128)(2,1)} reshape(bf16[16,72,2,4,576]{4,3,2,1,0:T(4,128)(2,1)} %copy.119) | data formatting | bytes 21233664 | tf_op jit(solution)/shard_map/reshape | solution.py:274
  681.1 15.8 fusion.70
  707.8 16.3 fusion.20
  735.5 24.9 %reshape.589 = bf16[16,72,2,4,576]{4,3,2,1,0:T(4,128)(2,1)} reshape(bf16[1152,4608]{1,0:T(8,128)(2,1)} %convolution_convert_fusion) | data formatting | bytes 21233664 | tf_op jit(solution)/shard_map/reshape | solution.py:293
  770.9 19.2 %reshape_reshape.7 = bf16[9216,576]{1,0:T(8,128)(2,1)} reshape(bf16[16,2,72,4,576]{4,3,2,1,0:T(4,128)(2,1)} %bitcast.312) | data formatting | bytes 21233664 | tf_op jit(solution)/shard_map/reshape;reshape | solution.py:308
  838.1 13.7 reshape.583
  851.9 21.3 %pad_maximum_fusion.2 = bf16[16,2,288,576]{3,1,2,0:T(2,128)(2,1)S(1)} fusion(bf16[16,2,72,576]{3,1,2,0:T(2,128)(2,1)S(1)} %bitcast.333, bf16[16,2,144,576]{3,1,2,0:T(2,128)(2,1)} %bitcast.327, bf16[16,2,72,576]{3,1,2,0:T(2,128)(2,1)} %bitcast.335), kind=kLoop, calls=%fused_computation.17 | loop fusion | flops 10616832 | bytes 21233664 | tf_op jit(solution)/shard_map/concatenate | solution.py:305
  901.5 18.8 %shard_map.282 = bf16[2,256,3456]{2,1,0:T(8,128)(2,1)S(1)} custom-call(s32[1]{0:T(128)} %bitcast.18.pair_ref, f32[2,256,3456]{2,1,0:T(8,128)} %bitcast.354, bf16[2,256,1152]{2,1,0:T(8,128)(2,1)S(1)} %bitcast.306, bf16[1152,128]{1,0:T(8,128)(2,1)S(1)} %copy-done.3), custom_call_target="tpu_custom_call" | custom-call | flops 4529848320 | bytes 16000000 | tf_op jit(solution)/shard_map/pallas_call | solution.py:139
  927.5 15.9 reshape.576
  943.3 34.5 %pad_maximum_fusion.1 = bf16[16,2,288,576]{3,1,2,0:T(2,128)(2,1)S(1)} fusion(bf16[16,2,72,576]{3,1,2,0:T(2,128)(2,1)} %bitcast.334, bf16[16,2,216,576]{3,1,2,0:T(2,128)(2,1)} %bitcast.315), kind=kLoop, calls=%fused_computation.16 | loop fusion | flops 5308416 | bytes 21233664 | tf_op jit(solution)/shard_map/concatenate | solution.py:305
  1027.3 11.7 convolution_convert_fusion.1
  1039.1 25.1 %reshape.588 = bf16[16,288,2,1,576]{4,2,1,0,3:T(2,128)(2,1)} reshape(bf16[4608,1152]{1,0:T(8,128)(2,1)} %convolution_convert_fusion.1) | data formatting | bytes 21233664 | tf_op jit(solution)/shard_map/reshape | solution.py:293
  1077.8 13.5 multiply_reduce_fusion
  1091.2 11.9 multiply_convert_fusion
  1160.4 16.1 reshape.563
  1176.5 60.3 %pad_maximum_fusion = bf16[16,2,304,576]{3,1,2,0:T(2,128)(2,1)S(1)} fusion(bf16[16,2,8,576]{3,1,2,0:T(2,128)(2,1)S(1)} %copy-done.49, bf16[16,2,8,576]{3,1,2,0:T(2,128)(2,1)} %copy.126, bf16[16,2,72,576]{3,1,2,0:T(2,128)(2,1)S(1)} %bitcast.332, bf16[16,2,216,576]{3,1,2,0:T(2,128)(2,1)} %bitcast.314), kind=kLoop, calls=%fused_computation.14 | loop fusion | flops 16809984 | bytes 22413312 | tf_op jit(solution)/shard_map/concatenate | solution.py:305
  1255.2 142.1 %reduce-scatter.12.cloned.1.call-done = bf16[288,576]{1,0:T(8,128)(2,1)} async-done(((bf16[9216,576]{1,0:T(8,128)(2,1)}), bf16[288,576]{1,0:T(8,128)(2,1)}) %reduce-scatter.12.cloned.1.call-update) | async-done | bytes 331792 | tf_op jit(solution)/shard_map/reduce_scatter | solution.py:307
  1399.2 269.6 %reduce-scatter.6.cloned.1.call-done = bf16[304,576]{1,0:T(8,128)(2,1)} async-done(((bf16[9728,576]{1,0:T(8,128)(2,1)}), bf16[304,576]{1,0:T(8,128)(2,1)}) %reduce-scatter.6.cloned.1.call-update) | async-done | bytes 350224 | tf_op jit(solution)/shard_map/reduce_scatter | solution.py:307
  (412 shorter events, 463.7 us)
Async XLA Ops:
  7.2 102.2 %all-gather.4.cloned.1.call-start = ((), (), s32[]{:S(2)}) async-start(), calls=%async_computation.5 | async-start | bytes 12840960 | tf_op jit(solution)/shard_map/all_gather | solution.py:263
  11.9 246.1 %all-gather.6.cloned.1.call-start = ((), (), s32[]{:S(2)}) async-start(), calls=%async_computation.6 | async-start | bytes 24330240 | tf_op jit(solution)/shard_map/all_gather | solution.py:263
  13.0 392.4 %all-gather.8.cloned.1.call-start = ((), (), s32[]{:S(2)}) async-start(), calls=%async_computation.7 | async-start | bytes 24330240 | tf_op jit(solution)/shard_map/all_gather | solution.py:263
  16.9 1231.0 %reduce-scatter.14.cloned.1.call-start = ((), (), s32[]{:S(2)}) async-start(), calls=%async_computation.12 | async-start | bytes 12165120 | tf_op jit(solution)/shard_map/reduce_scatter | solution.py:307
  22.3 621.0 %copy-start.2 = (bf16[1152,128]{1,0:T(8,128)(2,1)}, bf16[1152,128]{1,0:T(8,128)(2,1)S(1)}, u32[]{:S(2)}) copy-start(bf16[1152,128]{1,0:T(8,128)(2,1)S(1)} %fusion.38.ones_ref) | copy-start | bytes 884740
  126.0 41.1 %copy-start.63 = (f32[1152]{0:T(1024)}, f32[1152]{0:T(1024)S(1)}, u32[]{:S(2)}) copy-start(f32[1152]{0:T(1024)S(1)} %get-tuple-element.98) | copy-start | bytes 13828
  126.0 41.1 %copy-start.65 = (f32[1152]{0:T(1024)}, f32[1152]{0:T(1024)S(1)}, u32[]{:S(2)}) copy-start(f32[1152]{0:T(1024)S(1)} %get-tuple-element.99) | copy-start | bytes 13828
  126.0 57.3 %copy-start.67 = (f32[1152]{0:T(1024)}, f32[1152]{0:T(1024)S(1)}, u32[]{:S(2)}) copy-start(f32[1152]{0:T(1024)S(1)} %get-tuple-element.102) | copy-start | bytes 13828
  126.0 527.4 %copy-start.56 = (f32[1152]{0:T(1024)}, f32[1152]{0:T(1024)S(1)}, u32[]{:S(2)}) copy-start(f32[1152]{0:T(1024)S(1)} %get-tuple-element.97) | copy-start | bytes 13828
  489.9 12.4 copy-start.46
  509.0 153.5 %copy-start.34 = (bf16[120,2304]{0,1:T(8,128)(2,1)}, bf16[120,2304]{0,1:T(8,128)(2,1)S(1)}, u32[]{:S(2)}) copy-start(bf16[120,2304]{0,1:T(8,128)(2,1)S(1)} %copy.113) | copy-start | bytes 1658884
  668.2 39.6 %copy-start.79 = (f32[512]{0:T(512)}, f32[512]{0:T(512)S(1)}, u32[]{:S(2)}) copy-start(f32[512]{0:T(512)S(1)} %broadcast_multiply_fusion) | copy-start | bytes 6148
  669.6 11.5 slice-start.3
  669.9 37.8 %copy-start.92 = (f32[512]{0:T(512)}, f32[512]{0:T(512)S(1)}, u32[]{:S(2)}) copy-start(f32[512]{0:T(512)S(1)} %fusion.56) | copy-start | bytes 6148
  670.0 11.0 slice-start.4
  670.0 11.0 slice-start.5
  670.0 11.0 copy-start.51
  670.0 11.0 copy-start.71
  790.1 460.0 %reduce-scatter.10.cloned.1.call-start = ((), (), s32[]{:S(2)}) async-start(), calls=%async_computation.10 | async-start | bytes 12165120 | tf_op jit(solution)/shard_map/reduce_scatter | solution.py:307
  838.1 13.7 copy-start.11
  878.7 372.4 %reduce-scatter.8.cloned.1.call-start = ((), (), s32[]{:S(2)}) async-start(), calls=%async_computation.9 | async-start | bytes 12165120 | tf_op jit(solution)/shard_map/reduce_scatter | solution.py:307
  901.5 18.9 %copy-start.97 = (bf16[512,1152]{1,0:T(8,128)(2,1)S(1)}, bf16[512,1152]{1,0:T(8,128)(2,1)}, u32[]{:S(2)}) copy-start(bf16[512,1152]{1,0:T(8,128)(2,1)} %get-tuple-element.79) | copy-start | bytes 3538948
  983.6 413.7 %reduce-scatter.12.cloned.1.call-start = ((), (), s32[]{:S(2)}) async-start(), calls=%async_computation.11 | async-start | bytes 12165120 | tf_op jit(solution)/shard_map/reduce_scatter | solution.py:307
  1000.6 12.0 copy-start.38
  1075.8 593.0 %reduce-scatter.6.cloned.1.call-start = ((), (), s32[]{:S(2)}) async-start(), calls=%async_computation.8 | async-start | bytes 12840960 | tf_op jit(solution)/shard_map/reduce_scatter | solution.py:307
  1077.8 13.5 copy-start.54
  1103.1 15.5 slice-start.6
  1106.9 11.8 slice-start.7
  1108.4 17.4 %copy-start.17 = (bf16[16,72,512]{2,1,0:T(8,128)(2,1)}, bf16[16,72,512]{2,1,0:T(8,128)(2,1)S(1)}, u32[]{:S(2)}) copy-start(bf16[16,72,512]{2,1,0:T(8,128)(2,1)S(1)} %multiply_convert_fusion.4) | copy-start | bytes 3538948
  1133.2 15.5 copy-start.18
  1160.4 16.1 copy-start.10
  1160.4 16.1 copy-start.49
  (83 other events, 378.6 us)
Sparse Core Ops, SparseCore 0:
  12.0 97.3 all-gather.3
  112.9 144.9 all-gather.5
  260.9 144.5 all-gather.7
  790.2 146.6 reduce-scatter.13
  942.8 147.4 reduce-scatter.9
  1096.3 147.4 reduce-scatter.7
  1249.8 147.4 reduce-scatter.11
  1399.6 269.1 reduce-scatter.5
